TPU v7x, 32 devices: a whole 2x2x4 slice. The times are simulated.
32 devices in a mesh: light: 4 (over z), pix: 4 (over x, core), cam: 2 (over y).
Axes of the slice: x: 2, y: 2, z: 4, core: 2. Of those that a mesh axis runs over, the one named last changes fastest.
Arguments:
- reflectance: bfloat16 [1024, 32, 4096], P('light', 'cam', 'pix'), may hold values from -120 to 120
- start_basis: float32 [1024, 128], replicated, may hold values from -6 to 6
Outputs:
- core_tensor: float32 [128, 32, 4096], P('light', 'cam', 'pix')
- light_basis: float32 [1024, 128], P('light')
All inputs are finite; a program needn't handle non-finite values.
Results may differ from a plain program's by a relative error of at most 0.015.
Values may be sent and summed in bfloat16 or wider, within the bound.
A program may use at most 128 MiB of HBM per device.

v0:
```python
import jax
import jax.numpy as jnp
from jax import lax
from jax.sharding import PartitionSpec as P

ITERS = 2


def orthonormal(image_full):
    inner_gram = jnp.dot(
        image_full.T,
        image_full,
        preferred_element_type=jnp.float32,
        precision=lax.Precision.HIGHEST,
    )
    factor = jnp.linalg.cholesky(inner_gram)
    return lax.linalg.triangular_solve(
        factor, image_full, left_side=False, lower=True, transpose_a=True
    )


def per_device(reflectance, start_basis):
    light_rows, camera_cols, pixels = reflectance.shape
    rank_total = start_basis.shape[1]
    light_count = lax.axis_size("light")
    position = lax.axis_index("light")
    inverse_cols = 1.0 / (camera_cols * pixels * lax.axis_size("cam") * lax.axis_size("pix"))
    fibers = reflectance.reshape(light_rows, camera_cols * pixels)
    full_gram = None
    exchanged = None
    exchanged = lax.all_to_all(reflectance, "light", split_axis=2, concat_axis=0, tiled=True)
    gathered = exchanged.reshape(light_rows * light_count, -1)
    own_gram = lax.dot_general(
        gathered, gathered, (((1,), (1,)), ((), ())), preferred_element_type=jnp.float32
    )
    full_gram = lax.psum(own_gram, ("light", "pix", "cam")) * inverse_cols
    gram_rows = lax.dynamic_slice_in_dim(full_gram, position * light_rows, light_rows, 0)
    basis_now = start_basis
    for iteration in range(ITERS):
        image_rows = jnp.dot(
            gram_rows,
            basis_now,
            preferred_element_type=jnp.float32,
            precision=lax.Precision.HIGHEST,
        )
        image_full = lax.all_gather(
            image_rows.astype(jnp.bfloat16), "light", axis=0, tiled=True
        ).astype(image_rows.dtype)
        basis_now = orthonormal(image_full)
    basis_rows = lax.dynamic_slice_in_dim(basis_now, position * light_rows, light_rows, 0)
    rank_rows = rank_total // light_count
    rounded = basis_rows.astype(jnp.bfloat16)
    core_rows = lax.psum_scatter(
        lax.dot_general(
            rounded, fibers, (((0,), (0,)), ((), ())), preferred_element_type=jnp.float32
        ).astype(jnp.bfloat16),
        "light",
        scatter_dimension=0,
        tiled=True,
    ).astype(jnp.float32)
    return (core_rows.reshape(rank_rows, camera_cols, pixels), basis_rows)


def solution(mesh):
    placed = (P("light", "cam", "pix"), P())
    return jax.shard_map(
        per_device,
        mesh=mesh,
        in_specs=placed,
        out_specs=(P("light", "cam", "pix"), P("light", None)),
        check_vma=False,
    )
```

profile of v0, /device:TPU:0, one launch (start us, length us, event | category | flops | bytes accessed | tf_op | source)
XLA Modules:
  0.0 573.0 jit_solution(15910480420709180516)
XLA Ops:
  7.2 0.0 copy-start
  7.2 0.0 all-reduce.2.cloned.1.call-start
  7.2 13.4 %copy.16 = bf16[256,16,1024]{0,1,2:T(8,128)(2,1)} copy(bf16[256,16,1024]{2,1,0:T(8,128)(2,1)} %param.5) | data formatting | bytes 16777216 | tf_op args[0]
  20.7 192.2 %all_to_all.15 = bf16[256,16,1024]{0,1,2:T(8,128)(2,1)} all-to-all(bf16[256,16,1024]{0,1,2:T(8,128)(2,1)} %copy.16), channel_id=1, replica_groups=mesh['light'=4,'pix'=4,'cam'=2] {'light'}, dimensions={2} | all-to-all | bytes 16777216 | tf_op jit(solution)/shard_map/all_to_all | solution.py:31
  212.9 16.0 %copy.17 = bf16[256,16,4,256]{3,1,0,2:T(8,128)(2,1)} copy(bf16[256,16,4,256]{0,1,3,2:T(8,128)(2,1)} %bitcast.43) | data formatting | bytes 16777216 | tf_op jit(solution)/shard_map/all_to_all | solution.py:31
  228.9 12.2 %copy.21 = bf16[128,8,16,256]{3,1,2,0:T(8,128)(2,1)} copy(bf16[128,8,16,256]{3,2,1,0:T(8,128)(2,1)} %bitcast.44) | data formatting | bytes 16777216
  241.1 16.0 %fusion.17 = f32[1024,1024]{1,0:T(8,128)} fusion(bf16[1024,4096]{1,0:T(8,128)(2,1)} %bitcast.45), kind=kOutput, calls=%fused_computation.33 | convolution fusion | flops 8589934592 | bytes 12582912 | tf_op jit(solution)/shard_map/dot_general | solution.py:33
  257.1 0.0 all-reduce.2.cloned.1.call-update
  257.1 0.5 reduce-scatter.2.cloned.1.call-start
  257.7 15.6 %copy.22 = bf16[32,8,16,1024]{3,1,2,0:T(8,128)(2,1)} copy(bf16[32,8,16,1024]{3,2,1,0:T(8,128)(2,1)} %bitcast.41) | data formatting | bytes 16777216
  273.3 125.7 %all-reduce.2.cloned.1.call-done = f32[1024,1024]{1,0:T(8,128)} async-done(((f32[1024,1024]{1,0:T(8,128)}), f32[1024,1024]{1,0:T(8,128)}) %all-reduce.2.cloned.1.call-update) | async-done | bytes 4194320 | tf_op jit(solution)/shard_map/psum | solution.py:36
  399.0 0.0 copy-done
  399.0 2.2 convolution_convert_fusion.2
  401.2 14.5 %all_gather.6 = bf16[1024,128]{1,0:T(8,128)(2,1)S(1)} all-gather(bf16[256,128]{1,0:T(8,128)(2,1)S(1)} %convolution_convert_fusion.2), channel_id=1, replica_groups=mesh['light'=4,'pix'=4,'cam'=2] {'light'}, dimensions={0}, use_global_device_ids=true | all-gather | bytes 327680 | tf_op jit(solution)/shard_map/all_gather | solution.py:46
  415.7 0.3 fusion.18
  416.0 0.1 copy.18
  416.1 11.7 %cholesky.44 = f32[128,128]{1,0:T(8,128)S(1)} custom-call(f32[128,128]{1,0:T(8,128)S(1)} %fusion.9), custom_call_target="Cholesky" | custom-call | tf_op jit(solution)/shard_map/jit(cholesky)/cholesky | solution.py:16
  427.9 0.6 compare_reduce_fusion.1
  428.5 0.7 fusion.4
  429.2 9.8 %custom-call.6 = f32[1,128,128]{1,2,0:T(8,128)S(1)} custom-call(f32[1,128,128]{2,1,0:T(8,128)S(1)} %fusion.4), custom_call_target="InvertDiagBlocksLowerTriangular" | custom-call | tf_op jit(solution)/shard_map/triangular_solve/custom-call.0 | solution.py:17
  439.0 0.6 convolution_bitcast_fusion.1
  439.6 2.2 convolution_convert_fusion.1
  441.8 14.5 %all_gather.7 = bf16[1024,128]{1,0:T(8,128)(2,1)S(1)} all-gather(bf16[256,128]{1,0:T(8,128)(2,1)S(1)} %convolution_convert_fusion.1), channel_id=1, replica_groups=mesh['light'=4,'pix'=4,'cam'=2] {'light'}, dimensions={0}, use_global_device_ids=true | all-gather | bytes 327680 | tf_op jit(solution)/shard_map/all_gather | solution.py:46
  456.3 0.3 fusion.19
  456.6 0.1 copy.19
  456.7 11.7 %cholesky.55 = f32[128,128]{1,0:T(8,128)S(1)} custom-call(f32[128,128]{1,0:T(8,128)S(1)} %fusion.7), custom_call_target="Cholesky" | custom-call | tf_op jit(solution)/shard_map/jit(cholesky)/cholesky | solution.py:16
  468.4 0.6 compare_reduce_fusion
  469.1 0.7 fusion.5
  469.7 9.8 %custom-call.7 = f32[1,128,128]{1,2,0:T(8,128)S(1)} custom-call(f32[1,128,128]{2,1,0:T(8,128)S(1)} %fusion.5), custom_call_target="InvertDiagBlocksLowerTriangular" | custom-call | tf_op jit(solution)/shard_map/triangular_solve/custom-call.0 | solution.py:17
  479.6 0.6 convolution_bitcast_fusion
  480.2 6.6 %convolution_convert_fusion = bf16[128,16384]{1,0:T(8,128)(2,1)} fusion(bf16[256,16384]{1,0:T(8,128)(2,1)} %bitcast.42, f32[256,128]{0,1:T(8,128)S(1)} %constant_dynamic-slice_fusion), kind=kOutput, calls=%fused_computation | convolution fusion | flops 1075871744 | bytes 12713984 | tf_op jit(solution)/shard_map/dot_general | solution.py:54
  486.8 0.0 reduce-scatter.2.cloned.1.call-update
  486.9 0.8 copy.20
  487.6 75.2 %reduce-scatter.2.cloned.1.call-done = bf16[32,16384]{1,0:T(8,128)(2,1)} async-done(((bf16[128,16384]{1,0:T(8,128)(2,1)}), bf16[32,16384]{1,0:T(8,128)(2,1)}) %reduce-scatter.2.cloned.1.call-update) | async-done | bytes 1048592 | tf_op jit(solution)/shard_map/reduce_scatter | solution.py:53
  562.8 3.2 copy.23
  (5 shorter events, 0.1 us)
Async XLA Ops:
  7.2 391.9 %copy-start = (f32[1024,128]{1,0:T(8,128)S(1)}, f32[1024,128]{1,0:T(8,128)}, u32[]{:S(2)}) copy-start(f32[1024,128]{1,0:T(8,128)} %param.6) | copy-start | bytes 1572868
  7.2 391.8 %all-reduce.2.cloned.1.call-start = ((), (), s32[]{:S(2)}) async-start(), calls=%async_computation.2 | async-start | bytes 8388608 | tf_op jit(solution)/shard_map/psum | solution.py:36
  257.1 305.7 %reduce-scatter.2.cloned.1.call-start = ((), (), s32[]{:S(2)}) async-start(), calls=%async_computation.3 | async-start | bytes 5242880 | tf_op jit(solution)/shard_map/reduce_scatter | solution.py:53
Sparse Core Ops, SparseCore 0:
  257.3 141.7 all-reduce.1
  487.0 75.7 reduce-scatter.1
where the time goes:
time: 582 us; the launch traced here: 573 us
  blocking collectives  221 us (38%)
  waiting for transfers between devices  201 us (35%)
  local copies, waits for them, and re-layouts  61.5 us (11%)
  other arithmetic  45.7 us (8%)
  matrix products  28.8 us (5%)
  between operations  14.4 us (2%)
    all_to_all x1, blocking collectives, per_device(): lax.all_to_all(reflectance, 'light', split_axis=2, concat_axis=0, tiled=T...  192 us
    psum x1, waiting for transfers between devices, per_device(): full_gram = lax.psum(own_gram, ('light', 'pix', 'cam')) * inverse_cols  126 us
    reduce_scatter x1, waiting for transfers between devices, per_device(): lax.psum_scatter(lax.dot_general(rounded, fibers, (((0,), (0,)), ((), ())...  75.2 us
    unnamed x7, local copies, waits for them, and re-layouts  45.2 us
    all_gather x2, blocking collectives, per_device(): lax.all_gather(image_rows.astype(jnp.bfloat16), 'light', axis=0, tiled=True)  28.9 us
    another operation x6, other arithmetic, orthonormal(): factor = jnp.linalg.cholesky(inner_gram)  24.8 us
    another operation x4, other arithmetic, orthonormal(): lax.linalg.triangular_solve(factor, image_full, left_side=False, lower=Tr...  20.9 us
    all_to_all x1, local copies, waits for them, and re-layouts, per_device(): lax.all_to_all(reflectance, 'light', split_axis=2, concat_axis=0, tiled=T...  16 us
  transfers between devices with their start and end apart: 2, of which 2 were waited for; matrix products, arithmetic and copies ran while one was open for 3% of the time, Pallas kernels for 0%

commit v1 on v0

--- a/solution.py
+++ b/solution.py
@@ -33,7 +33,7 @@
     own_gram = lax.dot_general(
         gathered, gathered, (((1,), (1,)), ((), ())), preferred_element_type=jnp.float32
     )
-    full_gram = lax.psum(own_gram, ("light", "pix", "cam")) * inverse_cols
+    full_gram = lax.psum(lax.psum(own_gram, ("pix", "cam")), "light") * inverse_cols
     gram_rows = lax.dynamic_slice_in_dim(full_gram, position * light_rows, light_rows, 0)
     basis_now = start_basis
     for iteration in range(ITERS):

time: 582 us -> 677 us (1.16)
  waiting for transfers between devices: 201 us -> 296 us
    psum x1 -> x2, waiting for transfers between devices: 126 us -> 221 us  [the longest x1 141 us: per_device(): lax.psum(lax.psum(own_gram, ('pix', 'cam')), 'light') * inverse_cols]
  transfers between devices with their start and end apart: 2 -> 3, of which waited for: 2 -> 3; matrix products, arithmetic and copies ran while one was open for 3% -> 2% of each run, Pallas kernels for 0% -> 0%
where the time goes in v1:
time: 677 us; the launch traced here: 667 us
  waiting for transfers between devices  296 us (44%)
  blocking collectives  221 us (33%)
  local copies, waits for them, and re-layouts  61.5 us (9%)
  other arithmetic  45.7 us (7%)
  matrix products  28.8 us (4%)
  between operations  14.1 us (2%)
    all_to_all x1, blocking collectives, per_device(): lax.all_to_all(reflectance, 'light', split_axis=2, concat_axis=0, tiled=T...  192 us
    psum x1, waiting for transfers between devices, per_device(): lax.psum(lax.psum(own_gram, ('pix', 'cam')), 'light') * inverse_cols  141 us
    psum x1, waiting for transfers between devices, per_device(): lax.psum(own_gram, ('pix', 'cam'))  80 us
    reduce_scatter x1, waiting for transfers between devices, per_device(): lax.psum_scatter(lax.dot_general(rounded, fibers, (((0,), (0,)), ((), ())...  74.6 us
    unnamed x7, local copies, waits for them, and re-layouts  45.2 us
    all_gather x2, blocking collectives, per_device(): lax.all_gather(image_rows.astype(jnp.bfloat16), 'light', axis=0, tiled=True)  28.6 us
    another operation x6, other arithmetic, orthonormal(): factor = jnp.linalg.cholesky(inner_gram)  24.8 us
    another operation x4, other arithmetic, orthonormal(): lax.linalg.triangular_solve(factor, image_full, left_side=False, lower=Tr...  20.9 us
  transfers between devices with their start and end apart: 3, of which 3 were waited for; matrix products, arithmetic and copies ran while one was open for 2% of the time, Pallas kernels for 0%

profile of v1, /device:TPU:0, one launch (start us, length us, event | category | flops | bytes accessed | tf_op | source)
XLA Modules:
  0.0 667.5 jit_solution(9246464383742547681)
XLA Ops:
  7.2 0.0 copy-start
  7.2 0.0 all-reduce.3.cloned.1.call-start
  7.2 13.4 %copy.16 = bf16[256,16,1024]{0,1,2:T(8,128)(2,1)} copy(bf16[256,16,1024]{2,1,0:T(8,128)(2,1)} %param.5) | data formatting | bytes 16777216 | tf_op args[0]
  20.7 192.2 %all_to_all.15 = bf16[256,16,1024]{0,1,2:T(8,128)(2,1)} all-to-all(bf16[256,16,1024]{0,1,2:T(8,128)(2,1)} %copy.16), channel_id=1, replica_groups=mesh['light'=4,'pix'=4,'cam'=2] {'light'}, dimensions={2} | all-to-all | bytes 16777216 | tf_op jit(solution)/shard_map/all_to_all | solution.py:31
  212.9 16.0 %copy.17 = bf16[256,16,4,256]{3,1,0,2:T(8,128)(2,1)} copy(bf16[256,16,4,256]{0,1,3,2:T(8,128)(2,1)} %bitcast.43) | data formatting | bytes 16777216 | tf_op jit(solution)/shard_map/all_to_all | solution.py:31
  228.9 12.2 %copy.21 = bf16[128,8,16,256]{3,1,2,0:T(8,128)(2,1)} copy(bf16[128,8,16,256]{3,2,1,0:T(8,128)(2,1)} %bitcast.44) | data formatting | bytes 16777216
  241.1 16.0 %fusion.17 = f32[1024,1024]{1,0:T(8,128)} fusion(bf16[1024,4096]{1,0:T(8,128)(2,1)} %bitcast.45), kind=kOutput, calls=%fused_computation.33 | convolution fusion | flops 8589934592 | bytes 12582912 | tf_op jit(solution)/shard_map/dot_general | solution.py:33
  257.1 0.0 all-reduce.3.cloned.1.call-update
  257.1 0.0 all-reduce.5.cloned.1.call-start
  257.2 80.0 %all-reduce.3.cloned.1.call-done = f32[1024,1024]{1,0:T(8,128)} async-done(((f32[1024,1024]{1,0:T(8,128)}), f32[1024,1024]{1,0:T(8,128)}) %all-reduce.3.cloned.1.call-update) | async-done | bytes 4194320 | tf_op jit(solution)/shard_map/psum | solution.py:36
  337.2 0.0 all-reduce.5.cloned.1.call-update
  337.2 0.5 reduce-scatter.2.cloned.1.call-start
  337.8 15.6 %copy.22 = bf16[32,8,16,1024]{3,1,2,0:T(8,128)(2,1)} copy(bf16[32,8,16,1024]{3,2,1,0:T(8,128)(2,1)} %bitcast.41) | data formatting | bytes 16777216
  353.4 141.3 %all-reduce.5.cloned.1.call-done = f32[1024,1024]{1,0:T(8,128)} async-done(((f32[1024,1024]{1,0:T(8,128)}), f32[1024,1024]{1,0:T(8,128)}) %all-reduce.5.cloned.1.call-update) | async-done | bytes 4194320 | tf_op jit(solution)/shard_map/psum | solution.py:36
  494.7 0.0 copy-done
  494.7 2.2 convolution_convert_fusion.2
  496.9 14.5 %all_gather.6 = bf16[1024,128]{1,0:T(8,128)(2,1)S(1)} all-gather(bf16[256,128]{1,0:T(8,128)(2,1)S(1)} %convolution_convert_fusion.2), channel_id=1, replica_groups=mesh['light'=4,'pix'=4,'cam'=2] {'light'}, dimensions={0}, use_global_device_ids=true | all-gather | bytes 327680 | tf_op jit(solution)/shard_map/all_gather | solution.py:46
  511.4 0.3 fusion.18
  511.7 0.1 copy.18
  511.8 11.7 %cholesky.44 = f32[128,128]{1,0:T(8,128)S(1)} custom-call(f32[128,128]{1,0:T(8,128)S(1)} %fusion.9), custom_call_target="Cholesky" | custom-call | tf_op jit(solution)/shard_map/jit(cholesky)/cholesky | solution.py:16
  523.6 0.6 compare_reduce_fusion.1
  524.2 0.7 fusion.4
  524.9 9.8 %custom-call.6 = f32[1,128,128]{1,2,0:T(8,128)S(1)} custom-call(f32[1,128,128]{2,1,0:T(8,128)S(1)} %fusion.4), custom_call_target="InvertDiagBlocksLowerTriangular" | custom-call | tf_op jit(solution)/shard_map/triangular_solve/custom-call.0 | solution.py:17
  534.7 0.6 convolution_bitcast_fusion.1
  535.3 2.2 convolution_convert_fusion.1
  537.6 14.0 %all_gather.7 = bf16[1024,128]{1,0:T(8,128)(2,1)S(1)} all-gather(bf16[256,128]{1,0:T(8,128)(2,1)S(1)} %convolution_convert_fusion.1), channel_id=1, replica_groups=mesh['light'=4,'pix'=4,'cam'=2] {'light'}, dimensions={0}, use_global_device_ids=true | all-gather | bytes 327680 | tf_op jit(solution)/shard_map/all_gather | solution.py:46
  551.6 0.3 fusion.19
  551.9 0.1 copy.19
  552.0 11.7 %cholesky.55 = f32[128,128]{1,0:T(8,128)S(1)} custom-call(f32[128,128]{1,0:T(8,128)S(1)} %fusion.7), custom_call_target="Cholesky" | custom-call | tf_op jit(solution)/shard_map/jit(cholesky)/cholesky | solution.py:16
  563.7 0.6 compare_reduce_fusion
  564.4 0.7 fusion.5
  565.0 9.8 %custom-call.7 = f32[1,128,128]{1,2,0:T(8,128)S(1)} custom-call(f32[1,128,128]{2,1,0:T(8,128)S(1)} %fusion.5), custom_call_target="InvertDiagBlocksLowerTriangular" | custom-call | tf_op jit(solution)/shard_map/triangular_solve/custom-call.0 | solution.py:17
  574.9 0.6 convolution_bitcast_fusion
  575.5 6.6 convolution_convert_fusion
  582.1 0.0 reduce-scatter.2.cloned.1.call-update
  582.2 0.8 copy.20
  582.9 74.6 %reduce-scatter.2.cloned.1.call-done = bf16[32,16384]{1,0:T(8,128)(2,1)} async-done(((bf16[128,16384]{1,0:T(8,128)(2,1)}), bf16[32,16384]{1,0:T(8,128)(2,1)}) %reduce-scatter.2.cloned.1.call-update) | async-done | bytes 1048592 | tf_op jit(solution)/shard_map/reduce_scatter | solution.py:53
  657.5 3.2 copy.23
  (5 shorter events, 0.1 us)
Async XLA Ops:
  7.2 487.5 %copy-start = (f32[1024,128]{1,0:T(8,128)S(1)}, f32[1024,128]{1,0:T(8,128)}, u32[]{:S(2)}) copy-start(f32[1024,128]{1,0:T(8,128)} %param.6) | copy-start | bytes 1572868
  7.2 330.0 %all-reduce.3.cloned.1.call-start = ((), (), s32[]{:S(2)}) async-start(), calls=%async_computation.2 | async-start | bytes 8388608 | tf_op jit(solution)/shard_map/psum | solution.py:36
  257.1 237.5 %all-reduce.5.cloned.1.call-start = ((), (), s32[]{:S(2)}) async-start(), calls=%async_computation.3 | async-start | bytes 8388608 | tf_op jit(solution)/shard_map/psum | solution.py:36
  337.2 320.3 %reduce-scatter.2.cloned.1.call-start = ((), (), s32[]{:S(2)}) async-start(), calls=%async_computation.4 | async-start | bytes 5242880 | tf_op jit(solution)/shard_map/reduce_scatter | solution.py:53
Sparse Core Ops, SparseCore 0:
  257.3 79.9 all-reduce.2
  339.6 155.0 all-reduce.4
  582.3 75.2 reduce-scatter.1

commit v2 on v0

--- a/solution.py
+++ b/solution.py
@@ -28,7 +28,12 @@
     fibers = reflectance.reshape(light_rows, camera_cols * pixels)
     full_gram = None
     exchanged = None
-    exchanged = lax.all_to_all(reflectance, "light", split_axis=2, concat_axis=0, tiled=True)
+    exchanged = jnp.concatenate(
+        lax.all_to_all(
+            jnp.stack(jnp.split(reflectance, lax.axis_size("light"), axis=2)), "light", 0, 0
+        ),
+        axis=0,
+    )
     gathered = exchanged.reshape(light_rows * light_count, -1)
     own_gram = lax.dot_general(
         gathered, gathered, (((1,), (1,)), ((), ())), preferred_element_type=jnp.float32

time: 582 us -> 554 us (0.952)
  local copies, waits for them, and re-layouts: 61.5 us -> 35.9 us
    all_to_all x1 -> x0, local copies, waits for them, and re-layouts: 16 us -> none  [per_device(): lax.all_to_all(reflectance, 'light', split_axis=2, concat_axis=0, tiled=T...]
    unnamed x7 -> x6, local copies, waits for them, and re-layouts: 45.2 us -> 31.8 us
where the time goes in v2:
time: 554 us; the launch traced here: 546 us
  blocking collectives  218 us (39%)
  waiting for transfers between devices  201 us (36%)
  other arithmetic  46.9 us (8%)
  local copies, waits for them, and re-layouts  35.9 us (6%)
  matrix products  28.8 us (5%)
  between operations  14.4 us (3%)
    all_to_all x1, blocking collectives, per_device(): lax.all_to_all(jnp.stack(jnp.split(reflectance, lax.axis_size('light'), a...  189 us
    psum x1, waiting for transfers between devices, per_device(): full_gram = lax.psum(own_gram, ('light', 'pix', 'cam')) * inverse_cols  126 us
    reduce_scatter x1, waiting for transfers between devices, per_device(): lax.psum_scatter(lax.dot_general(rounded, fibers, (((0,), (0,)), ((), ())...  75.2 us
    unnamed x6, local copies, waits for them, and re-layouts  31.8 us
    all_gather x2, blocking collectives, per_device(): lax.all_gather(image_rows.astype(jnp.bfloat16), 'light', axis=0, tiled=True)  28.9 us
    another operation x6, other arithmetic, orthonormal(): factor = jnp.linalg.cholesky(inner_gram)  24.8 us
    another operation x4, other arithmetic, orthonormal(): lax.linalg.triangular_solve(factor, image_full, left_side=False, lower=Tr...  20.9 us
    dot_general x1, matrix products, per_device(): lax.dot_general(gathered, gathered, (((1,), (1,)), ((), ())), preferred_e...  16 us
  transfers between devices with their start and end apart: 2, of which 2 were waited for; matrix products, arithmetic and copies ran while one was open for 3% of the time, Pallas kernels for 0%

profile of v2, /device:TPU:0, one launch (start us, length us, event | category | flops | bytes accessed | tf_op | source)
XLA Modules:
  0.0 546.2 jit_solution(12962379802645633339)
XLA Ops:
  7.2 0.0 copy-start
  7.2 0.0 all-reduce.2.cloned.1.call-start
  7.2 3.9 slice_bitcast_fusion.3
  11.2 1.1 pad_maximum_fusion
  12.3 189.3 %all_to_all.5 = bf16[4,256,16,256]{3,2,1,0:T(8,128)(2,1)} all-to-all(bf16[4,256,16,256]{3,2,1,0:T(8,128)(2,1)S(1)} %pad_maximum_fusion), channel_id=1, replica_groups=mesh['light'=4,'pix'=4,'cam'=2] {'light'}, dimensions={0} | all-to-all | bytes 16777216 | tf_op jit(solution)/shard_map/all_to_all | solution.py:32
  201.6 12.2 %copy.7 = bf16[128,8,16,256]{3,1,2,0:T(8,128)(2,1)} copy(bf16[128,8,16,256]{3,2,1,0:T(8,128)(2,1)} %bitcast.49) | data formatting | bytes 16777216
  213.8 16.0 %fusion.17 = f32[1024,1024]{1,0:T(8,128)} fusion(bf16[1024,4096]{1,0:T(8,128)(2,1)} %bitcast.50), kind=kOutput, calls=%fused_computation.38 | convolution fusion | flops 8589934592 | bytes 12582912 | tf_op jit(solution)/shard_map/dot_general | solution.py:38
  229.8 0.0 all-reduce.2.cloned.1.call-update
  229.8 0.5 reduce-scatter.2.cloned.1.call-start
  230.3 15.6 %copy.8 = bf16[32,8,16,1024]{3,1,2,0:T(8,128)(2,1)} copy(bf16[32,8,16,1024]{3,2,1,0:T(8,128)(2,1)} %bitcast.47) | data formatting | bytes 16777216
  246.0 126.2 %all-reduce.2.cloned.1.call-done = f32[1024,1024]{1,0:T(8,128)} async-done(((f32[1024,1024]{1,0:T(8,128)}), f32[1024,1024]{1,0:T(8,128)}) %all-reduce.2.cloned.1.call-update) | async-done | bytes 4194320 | tf_op jit(solution)/shard_map/psum | solution.py:41
  372.2 0.0 copy-done
  372.2 2.2 convolution_convert_fusion.2
  374.4 14.5 %all_gather.6 = bf16[1024,128]{1,0:T(8,128)(2,1)S(1)} all-gather(bf16[256,128]{1,0:T(8,128)(2,1)S(1)} %convolution_convert_fusion.2), channel_id=1, replica_groups=mesh['light'=4,'pix'=4,'cam'=2] {'light'}, dimensions={0}, use_global_device_ids=true | all-gather | bytes 327680 | tf_op jit(solution)/shard_map/all_gather | solution.py:51
  388.9 0.3 fusion.18
  389.1 0.1 copy.4
  389.2 11.7 %cholesky.44 = f32[128,128]{1,0:T(8,128)S(1)} custom-call(f32[128,128]{1,0:T(8,128)S(1)} %fusion.9), custom_call_target="Cholesky" | custom-call | tf_op jit(solution)/shard_map/jit(cholesky)/cholesky | solution.py:16
  401.0 0.6 compare_reduce_fusion.1
  401.6 0.7 fusion.4
  402.3 9.8 %custom-call.6 = f32[1,128,128]{1,2,0:T(8,128)S(1)} custom-call(f32[1,128,128]{2,1,0:T(8,128)S(1)} %fusion.4), custom_call_target="InvertDiagBlocksLowerTriangular" | custom-call | tf_op jit(solution)/shard_map/triangular_solve/custom-call.0 | solution.py:17
  412.1 0.6 convolution_bitcast_fusion.1
  412.7 2.2 convolution_convert_fusion.1
  415.0 14.5 %all_gather.7 = bf16[1024,128]{1,0:T(8,128)(2,1)S(1)} all-gather(bf16[256,128]{1,0:T(8,128)(2,1)S(1)} %convolution_convert_fusion.1), channel_id=1, replica_groups=mesh['light'=4,'pix'=4,'cam'=2] {'light'}, dimensions={0}, use_global_device_ids=true | all-gather | bytes 327680 | tf_op jit(solution)/shard_map/all_gather | solution.py:51
  429.4 0.3 fusion.19
  429.7 0.1 copy.5
  429.8 11.7 %cholesky.55 = f32[128,128]{1,0:T(8,128)S(1)} custom-call(f32[128,128]{1,0:T(8,128)S(1)} %fusion.7), custom_call_target="Cholesky" | custom-call | tf_op jit(solution)/shard_map/jit(cholesky)/cholesky | solution.py:16
  441.6 0.6 compare_reduce_fusion
  442.2 0.7 fusion.5
  442.9 9.8 %custom-call.7 = f32[1,128,128]{1,2,0:T(8,128)S(1)} custom-call(f32[1,128,128]{2,1,0:T(8,128)S(1)} %fusion.5), custom_call_target="InvertDiagBlocksLowerTriangular" | custom-call | tf_op jit(solution)/shard_map/triangular_solve/custom-call.0 | solution.py:17
  452.7 0.6 convolution_bitcast_fusion
  453.3 6.6 %convolution_convert_fusion = bf16[128,16384]{1,0:T(8,128)(2,1)} fusion(bf16[256,16384]{1,0:T(8,128)(2,1)} %bitcast.48, f32[256,128]{0,1:T(8,128)S(1)} %constant_dynamic-slice_fusion), kind=kOutput, calls=%fused_computation | convolution fusion | flops 1075871744 | bytes 12713984 | tf_op jit(solution)/shard_map/dot_general | solution.py:59
  460.0 0.0 reduce-scatter.2.cloned.1.call-update
  460.0 0.8 copy.6
  460.7 75.2 %reduce-scatter.2.cloned.1.call-done = bf16[32,16384]{1,0:T(8,128)(2,1)} async-done(((bf16[128,16384]{1,0:T(8,128)(2,1)}), bf16[32,16384]{1,0:T(8,128)(2,1)}) %reduce-scatter.2.cloned.1.call-update) | async-done | bytes 1048592 | tf_op jit(solution)/shard_map/reduce_scatter | solution.py:58
  535.9 3.2 copy.9
  (5 shorter events, 0.1 us)
Async XLA Ops:
  7.2 365.0 %copy-start = (f32[1024,128]{1,0:T(8,128)S(1)}, f32[1024,128]{1,0:T(8,128)}, u32[]{:S(2)}) copy-start(f32[1024,128]{1,0:T(8,128)} %param.6) | copy-start | bytes 1572868
  7.2 365.0 %all-reduce.2.cloned.1.call-start = ((), (), s32[]{:S(2)}) async-start(), calls=%async_computation.2 | async-start | bytes 8388608 | tf_op jit(solution)/shard_map/psum | solution.py:41
  229.8 306.1 %reduce-scatter.2.cloned.1.call-start = ((), (), s32[]{:S(2)}) async-start(), calls=%async_computation.3 | async-start | bytes 5242880 | tf_op jit(solution)/shard_map/reduce_scatter | solution.py:58
Sparse Core Ops, SparseCore 0:
  229.9 142.1 all-reduce.1
  460.1 75.7 reduce-scatter.1
